TPU v7x, 256 devices: a whole 4x4x8 slice. The times are simulated.
256 devices in a mesh: row: 2 (over core), col: 64 (over z, y, x_hi), layer: 2 (over x_lo).
Axes of the slice: x: 4 (x_hi: 2, x_lo: 2; x = x_hi * 2 + x_lo), y: 4, z: 8, core: 2. Of those that a mesh axis runs over, the one named last changes fastest.
Arguments:
- flow_cols: int32 [16, 2, 64], P('row', 'layer', 'col'), may hold values from 0 to 64, as said below
- flow_vals: bfloat16 [16, 2, 64, 128, 128], P('row', 'layer', 'col'), may hold values from -22 to 22
- window_flow: bfloat16 [2, 8192, 32768], P('layer', 'row', 'col'), may hold values from -0.1403165 to 0.1403165
Outputs:
- flow_next: float32 [2048, 32768], P(('row', 'layer'), 'col')
Inputs may be any that keep to these rules, and one draw needn't show every extreme that they name: `flow_cols`: an entry 64 marks an empty slot; the live entries of one block row and layer are distinct; every block row and layer has at least one live slot, and some block row and layer has all 64 slots live.
All inputs are finite; a program needn't handle non-finite values.
Results may differ from a plain program's by a relative error of at most 0.0003.
Values may be sent and summed in bfloat16 or wider, within the bound.
A program may use at most 128 MiB of HBM per device.

v0:
```python
import jax
import jax.numpy as jnp
from jax import lax
from jax.sharding import PartitionSpec as P


def body(flow_cols, flow_vals, window_flow):
    row = lax.axis_index("row")
    layer = lax.axis_index("layer")
    n_layer = lax.axis_size("layer")
    own_g = window_flow[0]
    half_rows = own_g.shape[0]
    other_g = lax.ppermute(own_g, "row", perm=[(0, 1), (1, 0)])
    panel = jnp.zeros((2 * half_rows, own_g.shape[1]), own_g.dtype)
    panel = lax.dynamic_update_slice_in_dim(panel, own_g, row * half_rows, 0)
    panel = lax.dynamic_update_slice_in_dim(panel, other_g, (1 - row) * half_rows, 0)
    block_size = flow_vals.shape[-1]
    block_count = panel.shape[0] // block_size
    row_blocks = flow_vals.shape[0]
    wide_cols = jnp.broadcast_to(
        flow_cols.astype(jnp.bfloat16)[..., None, None], flow_cols.shape + (16, 128)
    )
    wide_cols = lax.optimization_barrier(wide_cols)
    slot_cols = lax.all_gather(wide_cols, "col", axis=2, tiled=True)[:, 0, :, 0, 0].astype(
        jnp.float32
    )
    slot_vals = lax.all_gather(flow_vals, "col", axis=2, tiled=True)[:, 0]
    column_ids = jnp.arange(block_count, dtype=jnp.float32)
    one_hot = (slot_cols[:, :, None] == column_ids[None, None, :]).astype(jnp.bfloat16)
    share = row_blocks // n_layer
    send_blocks = (1 - layer) * share
    keep_blocks = layer * share

    def expand(first_block):
        vals = lax.dynamic_slice_in_dim(slot_vals, first_block, share, 0)
        hot = lax.dynamic_slice_in_dim(one_hot, first_block, share, 0)
        dense = jnp.einsum("isab,isk->iakb", vals, hot, preferred_element_type=jnp.bfloat16)
        dense = dense.reshape(share * block_size, block_count * block_size)
        return jnp.dot(dense, panel, preferred_element_type=jnp.float32)

    sent = expand(send_blocks)
    received = lax.ppermute(sent, "layer", perm=[(0, 1), (1, 0)])
    summed = expand(keep_blocks) + received
    squares = summed * summed
    total_rows = row_blocks * block_size * lax.axis_size("row")
    column_sums = lax.psum(jnp.sum(squares, axis=0), ("row", "layer"))
    return squares / (column_sums / total_rows + 1e-06)


def solution(mesh):
    placed = (
        P("row", "layer", "col"),
        P("row", "layer", "col", None, None),
        P("layer", "row", "col"),
    )
    return jax.shard_map(
        body, mesh=mesh, in_specs=placed, out_specs=P(("row", "layer"), "col"), check_vma=False
    )
```

profile of v0, /device:TPU:1, one launch (start us, length us, event | category | flops | bytes accessed | tf_op | source)
XLA Modules:
  0.0 435.7 jit_solution(5035930560204560066)
XLA Ops:
  6.5 0.0 all-gather.3.cloned.1.call-start
  6.5 0.7 convert_bitcast_fusion
  7.2 0.7 broadcast_in_dim.7
  7.9 0.0 all-gather.3.cloned.1.call-update
  7.9 0.0 all-gather.5.cloned.1.call-start
  8.0 0.7 all-gather.5.cloned.1.call-update
  8.7 3.3 collective-permute-start
  12.0 0.0 copy-start
  12.0 4.2 broadcast_in_dim.16
  16.2 0.0 copy-done
  16.2 2.2 constant_dynamic-update-slice_fusion.1
  18.4 111.7 %all-gather.3.cloned.1.call-done = bf16[8,1,64,16,128]{4,3,1,0,2:T(8,128)(2,1)} async-done(((bf16[8,1,1,16,128]{4,3,1,0,2:T(8,128)(2,1)}), bf16[8,1,64,16,128]{4,3,1,0,2:T(8,128)(2,1)}) %all-gather.3.cloned.1.call-update) | async-done | bytes 2097168 | tf_op jit(solution)/shard_map/all_gather | solution.py:24
  130.1 1.4 slice.4
  131.5 0.2 copy.14
  131.6 0.1 iota_compare_fusion
  131.7 0.0 collective-permute-done
  131.7 4.4 %constant_dynamic-update-slice_fusion = bf16[8192,512]{1,0:T(8,128)(2,1)} fusion(bf16[8192,512]{1,0:T(8,128)(2,1)} %constant_dynamic-update-slice_fusion.1, bf16[4096,512]{1,0:T(8,128)(2,1)} %collective-permute-done, s32[]{:T(128)S(6)} %select_n.16), kind=kLoop, calls=%fused_computation.24 | loop fusion | bytes 8388612 | tf_op jit(solution)/shard_map/dynamic_update_slice | solution.py:16
  136.1 209.0 %all-gather.5.cloned.1.call-done = bf16[8,1,64,128,128]{4,3,2,1,0:T(8,128)(2,1)} async-done(((bf16[8,1,1,128,128]{4,3,2,1,0:T(8,128)(2,1)}), bf16[8,1,64,128,128]{4,3,2,1,0:T(8,128)(2,1)}) %all-gather.5.cloned.1.call-update) | async-done | bytes 16777232 | tf_op jit(solution)/shard_map/all_gather | solution.py:27
  345.1 9.4 %constant_dynamic-slice_fusion.1 = (bf16[4,1,64,128,128]{4,3,2,1,0:T(8,128)(2,1)S(1)}, bf16[4,1,64,128,128]{4,3,2,1,0:T(8,128)(2,1)}) fusion(bf16[8,1,64,128,128]{4,3,2,1,0:T(8,128)(2,1)} %all-gather.5.cloned.1.call-done, s32[]{:T(128)S(6)} %select_n.14, s32[]{:T(128)S(6)} %select_n.17), kind=kLoop, calls=%fused_computation.26 | loop fusion | bytes 33554440 | tf_op jit(solution)/shard_map/dynamic_slice | solution.py:35
  354.6 13.4 %fusion.6 = bf16[4,64,128,128]{3,1,2,0:T(8,128)(2,1)} fusion(bf16[4,1,64,128,128]{4,3,2,1,0:T(8,128)(2,1)} %get-tuple-element.6, pred[8,64,64]{1,2,0:T(32,128)(4,1)S(1)} %iota_compare_fusion, s32[]{:T(128)S(6)} %select_n.17), kind=kOutput, calls=%fused_computation.6 | convolution fusion | flops 536870912 | bytes 16809988 | tf_op jit(solution)/shard_map/isab,isk->iakb/dot_general | solution.py:37
  368.0 13.8 %fusion = f32[512,512]{1,0:T(8,128)S(1)} fusion(bf16[8192,512]{1,0:T(8,128)(2,1)} %constant_dynamic-update-slice_fusion, bf16[64,8,64,128]{3,2,1,0:T(8,128)(2,1)} %bitcast.44), kind=kOutput, calls=%fused_computation | convolution fusion | flops 4294967296 | bytes 17825792 | tf_op jit(solution)/shard_map/dot_general | solution.py:39
  381.8 0.4 collective-permute-start.1
  382.2 8.4 %fusion.8 = bf16[4,64,128,128]{3,1,2,0:T(8,128)(2,1)} fusion(bf16[4,1,64,128,128]{4,3,2,1,0:T(8,128)(2,1)S(1)} %get-tuple-element.5, pred[8,64,64]{1,2,0:T(32,128)(4,1)S(1)} %iota_compare_fusion, s32[]{:T(128)S(6)} %select_n.14), kind=kOutput, calls=%fused_computation.8 | convolution fusion | flops 536870912 | bytes 16809988 | tf_op jit(solution)/shard_map/isab,isk->iakb/dot_general | solution.py:37
  390.6 14.9 %collective-permute-done.1 = f32[512,512]{1,0:T(8,128)S(1)} collective-permute-done((f32[512,512]{1,0:T(8,128)S(1)}, f32[512,512]{1,0:T(8,128)S(1)}, u32[]{:S(2)}, u32[]{:S(2)}) %collective-permute-start.1) | collective-permute-done | bytes 1048608 | tf_op jit(solution)/shard_map/ppermute | solution.py:42
  405.5 13.8 %fusion.24 = (f32[512]{0:T(512)S(1)}, f32[512,512]{1,0:T(8,128)S(1)}) fusion(f32[512,512]{1,0:T(8,128)S(1)} %collective-permute-done.1, bf16[8192,512]{1,0:T(8,128)(2,1)} %constant_dynamic-update-slice_fusion, bf16[64,8,64,128]{3,2,1,0:T(8,128)(2,1)} %bitcast.43), kind=kOutput, calls=%fused_computation.29 | convolution fusion | flops 4295753216 | bytes 18876416 | tf_op jit(solution)/shard_map/dot_general | solution.py:39
  419.3 8.4 %psum.7 = f32[512]{0:T(512)S(1)} all-reduce(f32[512]{0:T(512)S(1)} %get-tuple-element.7), channel_id=1, replica_groups=mesh['row'=2,'col'=64,'layer'=2] {'row','layer'}, use_global_device_ids=true, to_apply=%region_1.0 | all-reduce | flops 512 | bytes 4096 | tf_op jit(solution)/shard_map/psum | solution.py:46
  427.7 1.1 broadcast_divide_fusion
  (2 shorter events, 0.0 us)
Async XLA Ops:
  6.5 123.5 %all-gather.3.cloned.1.call-start = ((), (), s32[]{:S(2)}) async-start(), calls=%async_computation | async-start | bytes 2129920 | tf_op jit(solution)/shard_map/all_gather | solution.py:24
  7.9 337.2 %all-gather.5.cloned.1.call-start = ((), (), s32[]{:S(2)}) async-start(), calls=%async_computation.1 | async-start | bytes 17039360 | tf_op jit(solution)/shard_map/all_gather | solution.py:27
  8.7 123.0 %collective-permute-start = (bf16[4096,512]{1,0:T(8,128)(2,1)}, bf16[4096,512]{1,0:T(8,128)(2,1)}, u32[]{:S(2)}, u32[]{:S(2)}) collective-permute-start(bf16[4096,512]{1,0:T(8,128)(2,1)} %bitcast.45), channel_id=1, source_target_pairs={{0,128},{128,0},{1,129},{129,1},{2,130},{130,2},{3,131},{131,3},{4... | collective-permute-start | bytes 12582920 | tf_op jit(solution)/shard_map/ppermute | solution.py:13
  12.0 4.2 copy-start
  381.8 23.7 %collective-permute-start.1 = (f32[512,512]{1,0:T(8,128)S(1)}, f32[512,512]{1,0:T(8,128)S(1)}, u32[]{:S(2)}, u32[]{:S(2)}) collective-permute-start(f32[512,512]{1,0:T(8,128)S(1)} %fusion), channel_id=1, source_target_pairs={{0,1},{1,0},{2,3},{3,2},{4,5},{5,4},{6,7},{7,6},{8,9},{9,8},{10,11... | collective-permute-start | bytes 3145736 | tf_op jit(solution)/shard_map/ppermute | solution.py:42
Sparse Core Ops, SparseCore 0:
  10.9 119.0 all-gather.2
  133.6 211.5 all-gather.4
where the time goes:
time: 436 us
  waiting for transfers between devices  336 us (77%)
  matrix products  49.5 us (11%)
  local copies, waits for them, and re-layouts  22.5 us (5%)
  between operations  13.4 us (3%)
  blocking collectives  8.44 us (2%)
    all_gather x1, waiting for transfers between devices, body(): slot_vals = lax.all_gather(flow_vals, 'col', axis=2, tiled=True)[:, 0]  209 us
    all_gather x1, waiting for transfers between devices, body(): lax.all_gather(wide_cols, 'col', axis=2, tiled=True)[:, 0, :, 0, 0]  112 us
    dot_general x2, matrix products, expand(): return jnp.dot(dense, panel, preferred_element_type=jnp.float32)  27.6 us
    dot_general x2, matrix products, expand(): jnp.einsum('isab,isk->iakb', vals, hot, preferred_element_type=jnp.bfloat16)  21.9 us
    ppermute x1, waiting for transfers between devices, body(): received = lax.ppermute(sent, 'layer', perm=[(0, 1), (1, 0)])  14.9 us
    dynamic_slice x1, local copies, waits for them, and re-layouts, expand(): vals = lax.dynamic_slice_in_dim(slot_vals, first_block, share, 0)  9.42 us
  transfers between devices with their start and end apart: 4, of which 3 were waited for; matrix products, arithmetic and copies ran while one was open for 5% of the time, Pallas kernels for 0%

commit v1 on v0

--- a/solution.py
+++ b/solution.py
@@ -2,6 +2,14 @@
 import jax.numpy as jnp
 from jax import lax
 from jax.sharding import PartitionSpec as P
+from jax.lax import all_to_all, axis_size
+
+map_signs = lambda mat, axis_id, which_dim: jnp.concatenate(
+    all_to_all(
+        jnp.stack(axis_size(axis_id) * [mat]), axis_name=axis_id, split_axis=0, concat_axis=0
+    ),
+    axis=which_dim,
+)
 
 
 def body(flow_cols, flow_vals, window_flow):
@@ -24,7 +32,7 @@
     slot_cols = lax.all_gather(wide_cols, "col", axis=2, tiled=True)[:, 0, :, 0, 0].astype(
         jnp.float32
     )
-    slot_vals = lax.all_gather(flow_vals, "col", axis=2, tiled=True)[:, 0]
+    slot_vals = map_signs(flow_vals, axis_id="col", which_dim=2)[:, 0]
     column_ids = jnp.arange(block_count, dtype=jnp.float32)
     one_hot = (slot_cols[:, :, None] == column_ids[None, None, :]).astype(jnp.bfloat16)
     share = row_blocks // n_layer

time: 436 us -> 512 us (1.17)
  waiting for transfers between devices: 336 us -> 387 us
  starting transfers between devices: 3.75 us -> 18.1 us
  local copies, waits for them, and re-layouts: 22.5 us -> 29.5 us
    all_gather x1 -> x0, waiting for transfers between devices: 209 us -> none  [body(): slot_vals = lax.all_gather(flow_vals, 'col', axis=2, tiled=True)[:, 0]]
    all_gather x1, waiting for transfers between devices: 112 us -> 253 us  [body(): lax.all_gather(wide_cols, 'col', axis=2, tiled=True)[:, 0, :, 0, 0]]
    all_to_all x0 -> x1, waiting for transfers between devices: none -> 120 us  [all_to_all(jnp.stack(axis_size(axis_id) * [mat]), axis_name=axis_id, spli...]
    another operation x0 -> x2, local copies, waits for them, and re-layouts: none -> 16.4 us
    all_to_all x0 -> x1, starting transfers between devices: none -> 15.5 us  [all_to_all(jnp.stack(axis_size(axis_id) * [mat]), axis_name=axis_id, spli...]
    dynamic_slice x1 -> x0, local copies, waits for them, and re-layouts: 9.42 us -> none  [expand(): vals = lax.dynamic_slice_in_dim(slot_vals, first_block, share, 0)]
  transfers between devices with their start and end apart: 4 -> 4, of which waited for: 3 -> 3; matrix products, arithmetic and copies ran while one was open for 5% -> 4% of each run, Pallas kernels for 0% -> 0%
where the time goes in v1:
time: 512 us; the launch traced here: 509 us
  waiting for transfers between devices  387 us (76%)
  matrix products  49.5 us (10%)
  local copies, waits for them, and re-layouts  29.5 us (6%)
  starting transfers between devices  18.1 us (4%)
  between operations  13.5 us (3%)
  blocking collectives  10.4 us (2%)
    all_gather x1, waiting for transfers between devices, body(): lax.all_gather(wide_cols, 'col', axis=2, tiled=True)[:, 0, :, 0, 0]  253 us
    all_to_all x1, waiting for transfers between devices, all_to_all(jnp.stack(axis_size(axis_id) * [mat]), axis_name=axis_id, spli...  120 us
    dot_general x2, matrix products, expand(): return jnp.dot(dense, panel, preferred_element_type=jnp.float32)  27.6 us
    dot_general x2, matrix products, expand(): jnp.einsum('isab,isk->iakb', vals, hot, preferred_element_type=jnp.bfloat16)  21.9 us
    all_to_all x1, starting transfers between devices, all_to_all(jnp.stack(axis_size(axis_id) * [mat]), axis_name=axis_id, spli...  15.5 us
    ppermute x1, waiting for transfers between devices, body(): received = lax.ppermute(sent, 'layer', perm=[(0, 1), (1, 0)])  12.9 us
    psum x1, blocking collectives, body(): column_sums = lax.psum(jnp.sum(squares, axis=0), ('row', 'layer'))  10.4 us
  transfers between devices with their start and end apart: 4, of which 3 were waited for; matrix products, arithmetic and copies ran while one was open for 4% of the time, Pallas kernels for 0%

profile of v1, /device:TPU:1, one launch (start us, length us, event | category | flops | bytes accessed | tf_op | source)
XLA Modules:
  0.0 508.7 jit_solution(9646576779558340475)
XLA Ops:
  6.5 6.9 %stack.2 = bf16[64,8,1,1,128,128]{5,4,1,3,2,0:T(8,128)(2,1)} broadcast(bf16[8,128,128]{2,1,0:T(8,128)(2,1)} %bitcast.51), dimensions={1,4,5} | broadcast | bytes 17039360 | tf_op jit(solution)/shard_map/stack | solution.py:9
  13.5 0.0 copy-start.1
  13.5 15.5 %all-to-all-start = ((bf16[64,8,1,1,128,128]{5,4,1,3,2,0:T(8,128)(2,1)}), bf16[64,8,1,1,128,128]{5,4,1,3,2,0:T(8,128)(2,1)}, u32[]{:S(2)}, u32[]{:S(2)}) async-start(bf16[64,8,1,1,128,128]{5,4,1,3,2,0:T(8,128)(2,1)} %stack.2), calls=%async_computation | async-start | bytes 33554432 | tf_op jit(solution)/shard_map/all_to_all | solution.py:8
  29.0 0.0 all-gather.2.cloned.1.call-start
  29.0 0.0 copy-done.1
  29.0 0.7 broadcast_in_dim.7
  29.7 0.0 all-gather.2.cloned.1.call-update
  29.8 1.0 collective-permute-start
  30.8 0.0 copy-start
  30.8 4.2 broadcast_in_dim.16
  35.0 0.0 copy-done
  35.0 2.2 constant_dynamic-update-slice_fusion.1
  37.2 253.2 %all-gather.2.cloned.1.call-done = bf16[8,1,64,16,128]{4,3,1,0,2:T(8,128)(2,1)} async-done(((bf16[8,1,1,16,128]{4,3,1,0,2:T(8,128)(2,1)}), bf16[8,1,64,16,128]{4,3,1,0,2:T(8,128)(2,1)}) %all-gather.2.cloned.1.call-update) | async-done | bytes 2097168 | tf_op jit(solution)/shard_map/all_gather | solution.py:32
  290.5 1.4 slice.4
  291.9 0.2 copy.12
  292.0 0.1 iota_compare_fusion
  292.1 0.0 collective-permute-done
  292.1 4.5 constant_dynamic-update-slice_fusion
  296.6 120.4 %all-to-all-done = bf16[64,8,1,1,128,128]{5,4,1,3,2,0:T(8,128)(2,1)} async-done(((bf16[64,8,1,1,128,128]{5,4,1,3,2,0:T(8,128)(2,1)}), bf16[64,8,1,1,128,128]{5,4,1,3,2,0:T(8,128)(2,1)}, u32[]{:S(2)}, u32[]{:S(2)}) %all-to-all-start) | async-done | bytes 16777248 | tf_op jit(solution)/shard_map/all_to_all | solution.py:8
  417.0 9.4 %constant_dynamic-slice_fusion.1 = (bf16[64,4,1,1,128,128]{5,4,1,3,2,0:T(8,128)(2,1)S(1)}, bf16[64,4,1,1,128,128]{5,4,1,3,2,0:T(8,128)(2,1)}) fusion(bf16[64,8,1,1,128,128]{5,4,1,3,2,0:T(8,128)(2,1)} %all-to-all-done, s32[]{:T(128)S(6)} %select_n.14, s32[]{:T(128)S(6)} %select_n.17), kind=kLoop, calls=%fused_computation.24 | loop fusion | bytes 33554440 | tf_op jit(solution)/shard_map/dynamic-slice.2
  426.4 13.4 %fusion.6 = bf16[4,64,128,128]{3,1,2,0:T(8,128)(2,1)} fusion(bf16[64,4,1,1,128,128]{5,4,1,3,2,0:T(8,128)(2,1)} %get-tuple-element.6, pred[8,64,64]{1,2,0:T(32,128)(4,1)S(1)} %iota_compare_fusion, s32[]{:T(128)S(6)} %select_n.17), kind=kOutput, calls=%fused_computation.7 | convolution fusion | flops 536870912 | bytes 16809988 | tf_op jit(solution)/shard_map/isab,isk->iakb/dot_general | solution.py:45
  439.8 13.8 %fusion = f32[512,512]{1,0:T(8,128)S(1)} fusion(bf16[8192,512]{1,0:T(8,128)(2,1)} %constant_dynamic-update-slice_fusion, bf16[64,8,64,128]{3,2,1,0:T(8,128)(2,1)} %bitcast.49), kind=kOutput, calls=%fused_computation | convolution fusion | flops 4294967296 | bytes 17825792 | tf_op jit(solution)/shard_map/dot_general | solution.py:47
  453.7 1.5 collective-permute-start.1
  455.2 8.4 %fusion.7 = bf16[4,64,128,128]{3,1,2,0:T(8,128)(2,1)} fusion(bf16[64,4,1,1,128,128]{5,4,1,3,2,0:T(8,128)(2,1)S(1)} %get-tuple-element.5, pred[8,64,64]{1,2,0:T(32,128)(4,1)S(1)} %iota_compare_fusion, s32[]{:T(128)S(6)} %select_n.14), kind=kOutput, calls=%fused_computation.9 | convolution fusion | flops 536870912 | bytes 16809988 | tf_op jit(solution)/shard_map/isab,isk->iakb/dot_general | solution.py:45
  463.6 12.9 %collective-permute-done.1 = f32[512,512]{1,0:T(8,128)S(1)} collective-permute-done((f32[512,512]{1,0:T(8,128)S(1)}, f32[512,512]{1,0:T(8,128)S(1)}, u32[]{:S(2)}, u32[]{:S(2)}) %collective-permute-start.1) | collective-permute-done | bytes 1048608 | tf_op jit(solution)/shard_map/ppermute | solution.py:50
  476.5 13.8 %fusion.20 = (f32[512]{0:T(512)S(1)}, f32[512,512]{1,0:T(8,128)S(1)}) fusion(f32[512,512]{1,0:T(8,128)S(1)} %collective-permute-done.1, bf16[8192,512]{1,0:T(8,128)(2,1)} %constant_dynamic-update-slice_fusion, bf16[64,8,64,128]{3,2,1,0:T(8,128)(2,1)} %bitcast.48), kind=kOutput, calls=%fused_computation.27 | convolution fusion | flops 4295753216 | bytes 18876416 | tf_op jit(solution)/shard_map/dot_general | solution.py:47
  490.3 10.4 %psum.7 = f32[512]{0:T(512)S(1)} all-reduce(f32[512]{0:T(512)S(1)} %get-tuple-element.7), channel_id=1, replica_groups=mesh['row'=2,'col'=64,'layer'=2] {'row','layer'}, use_global_device_ids=true, to_apply=%region_1.0 | all-reduce | flops 512 | bytes 4096 | tf_op jit(solution)/shard_map/psum | solution.py:54
  500.7 1.1 broadcast_divide_fusion
  (3 shorter events, 0.0 us)
Async XLA Ops:
  13.5 15.6 %copy-start.1 = (s32[8,1,1]{0,2,1:T(1,128)S(1)}, s32[8,1,1]{0,2,1:T(1,128)}, u32[]{:S(2)}) copy-start(s32[8,1,1]{0,2,1:T(1,128)} %param.3) | copy-start | bytes 100
  13.5 403.5 %all-to-all-start = ((bf16[64,8,1,1,128,128]{5,4,1,3,2,0:T(8,128)(2,1)}), bf16[64,8,1,1,128,128]{5,4,1,3,2,0:T(8,128)(2,1)}, u32[]{:S(2)}, u32[]{:S(2)}) async-start(bf16[64,8,1,1,128,128]{5,4,1,3,2,0:T(8,128)(2,1)} %stack.2), calls=%async_computation | async-start | bytes 33554432 | tf_op jit(solution)/shard_map/all_to_all | solution.py:8
  29.0 261.5 %all-gather.2.cloned.1.call-start = ((), (), s32[]{:S(2)}) async-start(), calls=%async_computation.1 | async-start | bytes 2129920 | tf_op jit(solution)/shard_map/all_gather | solution.py:32
  29.8 262.3 %collective-permute-start = (bf16[4096,512]{1,0:T(8,128)(2,1)}, bf16[4096,512]{1,0:T(8,128)(2,1)}, u32[]{:S(2)}, u32[]{:S(2)}) collective-permute-start(bf16[4096,512]{1,0:T(8,128)(2,1)} %bitcast.50), channel_id=1, source_target_pairs={{0,128},{128,0},{1,129},{129,1},{2,130},{130,2},{3,131},{131,3},{4... | collective-permute-start | bytes 12582920 | tf_op jit(solution)/shard_map/ppermute | solution.py:21
  30.8 4.2 copy-start
  453.7 22.9 %collective-permute-start.1 = (f32[512,512]{1,0:T(8,128)S(1)}, f32[512,512]{1,0:T(8,128)S(1)}, u32[]{:S(2)}, u32[]{:S(2)}) collective-permute-start(f32[512,512]{1,0:T(8,128)S(1)} %fusion), channel_id=1, source_target_pairs={{0,1},{1,0},{2,3},{3,2},{4,5},{5,4},{6,7},{7,6},{8,9},{9,8},{10,11... | collective-permute-start | bytes 3145736 | tf_op jit(solution)/shard_map/ppermute | solution.py:50
Sparse Core Ops, SparseCore 0:
  33.4 257.0 all-gather.1
